TPU v7x, 512 devices: a whole 4x8x8 slice. The times are simulated.
512 devices in a mesh: rep: 16 (over y_hi, x, core), shard: 32 (over y_lo, z).
Axes of the slice: x: 4, y: 8 (y_hi: 2, y_lo: 4; y = y_hi * 4 + y_lo), z: 8, core: 2. Of those that a mesh axis runs over, the one named last changes fastest.
Arguments:
- grad_blocks: float32 [16, 1664, 2048], P('rep', None, 'shard'), may hold values from -2400 to 2400
- gain_grads: float32 [16, 12800], P('rep', 'shard'), may hold values from -240 to 240
- first_moment: float32 [32, 106896], P('shard'), may hold values from -6 to 6
- second_moment: float32 [32, 106896], P('shard'), may hold values from 0.25 to 4
- master_flat: float32 [32, 106896], P('shard'), may hold values from -6 to 6
- ema_flat: float32 [32, 106896], P('shard'), may hold values from -6 to 6
Outputs:
- new_first: float32 [32, 106896], P('shard')
- new_second: float32 [32, 106896], P('shard')
- new_master: float32 [32, 106896], P('shard')
- new_ema: float32 [32, 106896], P('shard')
- weight_blocks: bfloat16 [2, 1664, 2048], P(None, None, 'shard')
- gains: bfloat16 [12800], replicated
All inputs are finite; a program needn't handle non-finite values.
Results may differ from a plain program's by a relative error of at most 0.0004.
Values may be sent and summed in bfloat16 or wider, within the bound.
A program may use at most 64 MiB of HBM per device.

v0:
```python
import jax
import jax.numpy as jnp
from jax import lax
from jax.sharding import PartitionSpec as P

STEP = 100
PARAMS = 3420672
beta_one = 0.9
beta_two = 0.95
adam_eps = 1e-08
learn_rate = 0.02
weight_decay = 0.1
ema_keep = 0.95
clip_eps = 1e-06


def shards(grad_blocks, gain_grads, first_moment, second_moment, master_flat, ema_flat):
    replicas = lax.axis_size("rep")
    matrix_part = grad_blocks[0]
    small_part = gain_grads[0]
    matrix_part, small_part = lax.psum((matrix_part, small_part), "rep")
    owned = lax.all_to_all(matrix_part, "shard", split_axis=0, concat_axis=1, tiled=True)
    partial_value = jnp.sum(owned * owned) + jnp.sum(small_part * small_part)
    total = lax.psum(partial_value, "shard") / (replicas * replicas)
    main_len = owned.shape[0] * owned.shape[1]
    grads = jnp.concatenate([owned.reshape(main_len), small_part]).reshape(1, -1) / replicas
    rms = jnp.sqrt(total / PARAMS)
    clip = jnp.minimum(1.0, 1.0 / (rms + clip_eps))
    clipped = grads * clip
    new_first = beta_one * first_moment + (1.0 - beta_one) * clipped
    new_second = beta_two * second_moment + (1.0 - beta_two) * clipped * clipped
    update = (
        new_first
        / (1.0 - beta_one**STEP)
        / (jnp.sqrt(new_second / (1.0 - beta_two**STEP)) + adam_eps)
    )
    column = jnp.arange(grads.shape[1], dtype=jnp.int32)[None, :]
    decayed = jnp.where(column < main_len, weight_decay * master_flat, 0.0)
    new_master = master_flat - learn_rate * (update + decayed)
    new_ema = ema_keep * ema_flat + (1.0 - ema_keep) * new_master
    weights = new_master[0, :main_len].reshape(owned.shape).astype(jnp.bfloat16)
    averaged = new_ema[0, :main_len].reshape(owned.shape).astype(jnp.bfloat16)
    stacked = jnp.stack([weights, averaged], axis=0)
    weight_blocks = lax.all_to_all(stacked, "shard", split_axis=2, concat_axis=1, tiled=True)
    gains = lax.all_gather(
        new_master[0, main_len:].astype(jnp.bfloat16), "shard", axis=0, tiled=True
    )
    return (new_first, new_second, new_master, new_ema, weight_blocks, gains)


def solution(mesh):
    return jax.shard_map(
        shards,
        mesh=mesh,
        in_specs=(
            P("rep", None, "shard"),
            P("rep", "shard"),
            P("shard", None),
            P("shard", None),
            P("shard", None),
            P("shard", None),
        ),
        out_specs=(
            P("shard", None),
            P("shard", None),
            P("shard", None),
            P("shard", None),
            P(None, None, "shard"),
            P(),
        ),
        check_vma=False,
    )
```

profile of v0, /device:TPU:32, one launch (start us, length us, event | category | flops | bytes accessed | tf_op | source)
XLA Modules:
  0.0 537.8 jit_solution(15047340786175874549)
XLA Ops:
  7.2 0.0 all-reduce.3.cloned.1.call-start
  7.2 3.5 all_to_all.25
  10.8 0.0 all-reduce.3.cloned.1.call-update
  10.8 188.7 %all-reduce.3.cloned.1.call-done = f32[32,52,64]{1,0,2:T(8,128)} async-done(((f32[32,52,64]{1,0,2:T(8,128)}), f32[32,52,64]{1,0,2:T(8,128)}) %all-reduce.3.cloned.1.call-update) | async-done | bytes 426000 | tf_op jit(solution)/shard_map/psum | solution.py:21
  199.4 1.8 copy.33
  201.3 0.0 copy-start.7
  201.3 1.3 reshape.115
  202.6 8.0 %all-to-all-start = ((f32[32,1,3328]{2,1,0:T(1,128)}), f32[32,1,3328]{2,1,0:T(1,128)S(1)}, u32[]{:S(2)}, u32[]{:S(2)}) async-start(f32[32,1,3328]{2,1,0:T(1,128)} %reshape.115), calls=%async_computation | async-start | bytes 851968 | tf_op jit(solution)/shard_map/all_to_all | solution.py:22
  210.6 0.0 copy-done.7
  210.6 48.1 %psum.22 = f32[400]{0:T(512)S(1)} all-reduce(f32[400]{0:T(512)S(1)} %bitcast.23), channel_id=1, replica_groups=mesh['rep'=16,'shard'=32] {'rep'}, use_global_device_ids=true, to_apply=%region_1.0 | all-reduce | flops 400 | bytes 3200 | tf_op jit(solution)/shard_map/psum | solution.py:21
  258.7 0.6 multiply_reduce_fusion.1
  259.3 0.0 all-to-all-done
  259.3 0.5 broadcast.66
  259.8 1.6 reduce.7
  261.4 0.3 reshape.116
  261.7 0.8 multiply_reduce_fusion
  263.8 80.5 %psum.23 = f32[]{:T(128)} all-reduce(f32[]{:T(128)S(6)} %add.30), channel_id=1, replica_groups=mesh['rep'=16,'shard'=32] {'shard'}, use_global_device_ids=true, to_apply=%region_4.0 | all-reduce | flops 1 | bytes 8 | tf_op jit(solution)/shard_map/psum | solution.py:24
  345.1 0.0 copy-start.6
  345.1 0.2 copy.34
  345.3 0.0 copy-start.4
  345.3 0.0 copy-start.5
  345.3 0.5 concatenate.18
  345.8 0.3 copy-done.6
  346.1 0.2 copy-done.4
  346.3 0.1 copy-done.5
  346.4 5.0 fusion.3
  351.4 0.0 copy-start.1
  351.4 0.0 copy-start
  351.4 0.0 copy-start.3
  351.4 0.7 copy-done.1
  352.2 1.2 slice_reduce_fusion
  353.4 0.1 convert_element_type.26
  353.5 0.0 copy-done.3
  353.5 0.7 multiply_add_fusion
  354.3 0.0 copy-done
  354.3 0.0 copy-start.2
  354.3 0.7 copy-done.2
  355.1 1.1 fusion.2
  356.2 0.1 convert_element_type.27
  356.3 0.8 copy.36
  357.1 0.8 copy.35
  358.0 2.8 fusion.5
  360.8 3.5 reshape.117
  364.3 3.9 all-to-all-start.1
  368.2 1.3 dynamic-slice
  370.2 0.7 slice_reduce_fusion.1
  370.9 0.3 dynamic-update-slice
  371.1 153.1 %all-reduce = bf16[12800]{0:T(1024)(128)(2,1)} all-reduce(bf16[12800]{0:T(1024)(128)(2,1)S(1)} %dynamic-update-slice), channel_id=2, replica_groups=mesh['rep'=16,'shard'=32] {'shard'}, use_global_device_ids=true, to_apply=%add | all-reduce | flops 12800 | bytes 51200 | tf_op jit(solution)/shard_map/all_gather | solution.py:45
  524.2 0.0 all-to-all-done.1
  524.2 3.3 reshape.118
  527.6 0.7 copy.42
  528.3 2.7 all_to_all.31
  (1 shorter events, 0.0 us)
Async XLA Ops:
  7.2 192.3 %all-reduce.3.cloned.1.call-start = ((), (), s32[]{:S(2)}) async-start(), calls=%async_computation.2 | async-start | bytes 2097152 | tf_op jit(solution)/shard_map/psum | solution.py:21
  201.3 9.3 %copy-start.7 = (f32[1,400]{1,0:T(1,128)S(1)}, f32[1,400]{1,0:T(1,128)}, u32[]{:S(2)}) copy-start(f32[1,400]{1,0:T(1,128)} %param.7) | copy-start | bytes 4804
  202.6 56.7 %all-to-all-start = ((f32[32,1,3328]{2,1,0:T(1,128)}), f32[32,1,3328]{2,1,0:T(1,128)S(1)}, u32[]{:S(2)}, u32[]{:S(2)}) async-start(f32[32,1,3328]{2,1,0:T(1,128)} %reshape.115), calls=%async_computation | async-start | bytes 851968 | tf_op jit(solution)/shard_map/all_to_all | solution.py:22
  345.1 1.0 copy-start.6
  345.3 1.0 copy-start.4
  345.3 1.2 copy-start.5
  351.4 0.8 copy-start.1
  351.4 2.9 copy-start
  351.4 2.1 copy-start.3
  354.3 0.8 copy-start.2
  364.3 159.9 %all-to-all-start.1 = ((bf16[32,2,3328]{2,1,0:T(2,128)(2,1)}), bf16[32,2,3328]{2,1,0:T(2,128)(2,1)S(1)}, u32[]{:S(2)}, u32[]{:S(2)}) async-start(bf16[32,2,3328]{2,1,0:T(2,128)(2,1)} %reshape.117), calls=%async_computation.1 | async-start | bytes 851968 | tf_op jit(solution)/shard_map/all_to_all | solution.py:44
Sparse Core Ops, SparseCore 0:
  10.9 188.4 all-reduce.2
where the time goes:
time: 538 us
  blocking collectives  282 us (52%)
  waiting for transfers between devices  189 us (35%)
  local copies, waits for them, and re-layouts  26.9 us (5%)
  between operations  16.9 us (3%)
  starting transfers between devices  11.9 us (2%)
  other arithmetic  11.6 us (2%)
    psum x1, waiting for transfers between devices, shards(): matrix_part, small_part = lax.psum((matrix_part, small_part), 'rep')  189 us
    all_gather x1, blocking collectives, shards(): lax.all_gather(new_master[0, main_len:].astype(jnp.bfloat16), 'shard', ax...  153 us
    psum x1, blocking collectives, shards(): total = lax.psum(partial_value, 'shard') / (replicas * replicas)  80.5 us
    psum x1, blocking collectives, shards(): matrix_part, small_part = lax.psum((matrix_part, small_part), 'rep')  48.1 us
    unnamed x23, local copies, waits for them, and re-layouts  12.1 us
  transfers between devices with their start and end apart: 3, of which 1 were waited for; matrix products, arithmetic and copies ran while one was open for 1% of the time, Pallas kernels for 0%

commit v1 on v0

--- a/solution.py
+++ b/solution.py
@@ -42,8 +42,14 @@
     averaged = new_ema[0, :main_len].reshape(owned.shape).astype(jnp.bfloat16)
     stacked = jnp.stack([weights, averaged], axis=0)
     weight_blocks = lax.all_to_all(stacked, "shard", split_axis=2, concat_axis=1, tiled=True)
-    gains = lax.all_gather(
-        new_master[0, main_len:].astype(jnp.bfloat16), "shard", axis=0, tiled=True
+    gains = jnp.concatenate(
+        lax.all_to_all(
+            jnp.stack([new_master[0, main_len:].astype(jnp.bfloat16)] * lax.axis_size("shard")),
+            "shard",
+            0,
+            0,
+        ),
+        axis=0,
     )
     return (new_first, new_second, new_master, new_ema, weight_blocks, gains)
 

time: 538 us -> 408 us (0.76)
  the two profiles are of different devices: /device:TPU:32 before, /device:TPU:64 now
where the time goes in v1:
time: 408 us; the launch traced here: 407 us
  waiting for transfers between devices  200 us (49%)
  blocking collectives  124 us (30%)
  starting transfers between devices  28.2 us (7%)
  local copies, waits for them, and re-layouts  26.1 us (6%)
  between operations  16.3 us (4%)
  other arithmetic  12.6 us (3%)
    psum x1, waiting for transfers between devices, shards(): matrix_part, small_part = lax.psum((matrix_part, small_part), 'rep')  189 us
    psum x1, blocking collectives, shards(): total = lax.psum(partial_value, 'shard') / (replicas * replicas)  76.4 us
    psum x1, blocking collectives, shards(): matrix_part, small_part = lax.psum((matrix_part, small_part), 'rep')  47.7 us
    all_to_all x1, waiting for transfers between devices, shards(): lax.all_to_all(stacked, 'shard', split_axis=2, concat_axis=1, tiled=True)  10.8 us
    unnamed x20, local copies, waits for them, and re-layouts  10.6 us
    all_to_all x1, starting transfers between devices, shards(): lax.all_to_all(stacked, 'shard', split_axis=2, concat_axis=1, tiled=True)  10.3 us
    all_to_all x1, starting transfers between devices, shards(): lax.all_to_all(matrix_part, 'shard', split_axis=0, concat_axis=1, tiled=T...  9.92 us
  transfers between devices with their start and end apart: 4, of which 2 were waited for; matrix products, arithmetic and copies ran while one was open for 3% of the time, Pallas kernels for 0%

profile of v1, /device:TPU:64, one launch (start us, length us, event | category | flops | bytes accessed | tf_op | source)
XLA Modules:
  0.0 407.1 jit_solution(3982760112405161947)
XLA Ops:
  7.2 0.0 all-reduce.2.cloned.1.call-start
  7.2 3.5 all_to_all.29
  10.8 0.0 all-reduce.2.cloned.1.call-update
  10.8 189.0 %all-reduce.2.cloned.1.call-done = f32[32,52,64]{1,0,2:T(8,128)} async-done(((f32[32,52,64]{1,0,2:T(8,128)}), f32[32,52,64]{1,0,2:T(8,128)}) %all-reduce.2.cloned.1.call-update) | async-done | bytes 426000 | tf_op jit(solution)/shard_map/psum | solution.py:21
  199.8 1.8 copy.33
  201.6 0.0 copy-start.6
  201.6 1.3 reshape.120
  202.9 9.9 %all-to-all-start = ((f32[32,1,3328]{2,1,0:T(1,128)}), f32[32,1,3328]{2,1,0:T(1,128)S(1)}, u32[]{:S(2)}, u32[]{:S(2)}) async-start(f32[32,1,3328]{2,1,0:T(1,128)} %reshape.120), calls=%async_computation | async-start | bytes 851968 | tf_op jit(solution)/shard_map/all_to_all | solution.py:22
  212.8 0.0 copy-done.6
  212.8 47.7 %psum.22 = f32[400]{0:T(512)S(1)} all-reduce(f32[400]{0:T(512)S(1)} %bitcast.22), channel_id=1, replica_groups=mesh['rep'=16,'shard'=32] {'rep'}, use_global_device_ids=true, to_apply=%region_1.0 | all-reduce | flops 400 | bytes 3200 | tf_op jit(solution)/shard_map/psum | solution.py:21
  260.5 0.6 multiply_reduce_fusion.1
  261.1 0.0 all-to-all-done
  261.1 0.5 broadcast.71
  261.7 1.6 reduce.8
  263.3 0.3 reshape.121
  263.6 0.8 multiply_reduce_fusion
  265.7 76.4 %psum.23 = f32[]{:T(128)} all-reduce(f32[]{:T(128)S(6)} %add.30), channel_id=1, replica_groups=mesh['rep'=16,'shard'=32] {'shard'}, use_global_device_ids=true, to_apply=%region_4.0 | all-reduce | flops 1 | bytes 8 | tf_op jit(solution)/shard_map/psum | solution.py:24
  342.8 0.0 copy-start.5
  342.8 0.2 copy.34
  343.0 0.0 copy-start.3
  343.0 0.0 copy-start.4
  343.0 0.5 concatenate.18
  343.6 0.3 copy-done.5
  343.8 0.2 copy-done.3
  344.1 0.1 copy-done.4
  344.2 5.0 %fusion.3 = (bf16[1,106896]{1,0:T(2,128)(2,1)S(1)}, f32[1,106896]{1,0:T(1,128)S(1)}, f32[1,106896]{1,0:T(1,128)}, f32[1,106896]{1,0:T(1,128)}) fusion(f32[1,106896]{1,0:T(1,128)S(1)} %copy-done.3, f32[]{:T(128)S(6)} %mul.88, f32[1,400]{1,0:T(1,128)S(1)} %bitcast.21, f32[1,106496]{1,0:T(1,128)S(1)} %concatenate.18, f32[1,106896]{1,0:T(1,128)S(1)} %copy-done.4, ...), kind=kLoop, calls=%fused_computation.16 | loop fusion | flops 2137920 | bytes 3206884 | tf_op jit(solution)/shard_map/convert.2
  349.2 0.0 copy-start
  349.2 0.0 copy-start.2
  349.2 1.2 slice_reduce_fusion
  350.4 0.1 convert_element_type.26
  350.6 0.5 broadcast.72
  351.1 0.8 reduce.9
  351.9 0.7 reshape.124
  352.6 8.0 %all-to-all-start.2 = ((bf16[32,2,200]{2,1,0:T(2,128)(2,1)}), bf16[32,2,200]{2,1,0:T(2,128)(2,1)S(1)}, u32[]{:S(2)}, u32[]{:S(2)}) async-start(bf16[32,2,200]{2,1,0:T(2,128)(2,1)} %reshape.124), calls=%async_computation.2 | async-start | bytes 65536 | tf_op jit(solution)/shard_map/all_to_all | solution.py:46
  360.7 0.0 copy-done.2
  360.7 0.7 multiply_add_fusion
  361.4 0.0 copy-done
  361.4 0.0 copy-start.1
  361.4 0.7 copy-done.1
  362.2 1.1 fusion.2
  363.3 0.1 convert_element_type.27
  363.4 0.8 copy.36
  364.3 0.8 copy.35
  365.1 2.8 fusion.5
  367.9 3.5 reshape.122
  371.5 0.0 all-to-all-done.2
  371.5 10.3 %all-to-all-start.1 = ((bf16[32,2,3328]{2,1,0:T(2,128)(2,1)}), bf16[32,2,3328]{2,1,0:T(2,128)(2,1)S(1)}, u32[]{:S(2)}, u32[]{:S(2)}) async-start(bf16[32,2,3328]{2,1,0:T(2,128)(2,1)} %reshape.122), calls=%async_computation.1 | async-start | bytes 851968 | tf_op jit(solution)/shard_map/all_to_all | solution.py:44
  381.7 0.1 reshape.125
  381.8 0.2 reduce.4
  382.0 0.7 reshape.114
  382.8 10.8 %all-to-all-done.1 = bf16[32,2,3328]{2,1,0:T(2,128)(2,1)S(1)} async-done(((bf16[32,2,3328]{2,1,0:T(2,128)(2,1)}), bf16[32,2,3328]{2,1,0:T(2,128)(2,1)S(1)}, u32[]{:S(2)}, u32[]{:S(2)}) %all-to-all-start.1) | async-done | bytes 426016 | tf_op jit(solution)/shard_map/all_to_all | solution.py:44
  393.6 3.3 reshape.123
  396.9 0.7 copy.42
  397.6 2.7 all_to_all.35
  (2 shorter events, 0.1 us)
Async XLA Ops:
  7.2 192.6 %all-reduce.2.cloned.1.call-start = ((), (), s32[]{:S(2)}) async-start(), calls=%async_computation.3 | async-start | bytes 2097152 | tf_op jit(solution)/shard_map/psum | solution.py:21
  201.6 11.2 %copy-start.6 = (f32[1,400]{1,0:T(1,128)S(1)}, f32[1,400]{1,0:T(1,128)}, u32[]{:S(2)}) copy-start(f32[1,400]{1,0:T(1,128)} %param.7) | copy-start | bytes 4804
  202.9 58.2 %all-to-all-start = ((f32[32,1,3328]{2,1,0:T(1,128)}), f32[32,1,3328]{2,1,0:T(1,128)S(1)}, u32[]{:S(2)}, u32[]{:S(2)}) async-start(f32[32,1,3328]{2,1,0:T(1,128)} %reshape.120), calls=%async_computation | async-start | bytes 851968 | tf_op jit(solution)/shard_map/all_to_all | solution.py:22
  342.8 1.0 copy-start.5
  343.0 1.0 copy-start.3
  343.0 1.2 copy-start.4
  349.2 12.2 %copy-start = (f32[1,106896]{1,0:T(1,128)}, f32[1,106896]{1,0:T(1,128)S(1)}, u32[]{:S(2)}) copy-start(f32[1,106896]{1,0:T(1,128)S(1)} %get-tuple-element.7) | copy-start | bytes 1282756
  349.2 11.5 %copy-start.2 = (f32[1,106896]{1,0:T(1,128)S(1)}, f32[1,106896]{1,0:T(1,128)}, u32[]{:S(2)}) copy-start(f32[1,106896]{1,0:T(1,128)} %param.11) | copy-start | bytes 1282756
  352.6 18.8 %all-to-all-start.2 = ((bf16[32,2,200]{2,1,0:T(2,128)(2,1)}), bf16[32,2,200]{2,1,0:T(2,128)(2,1)S(1)}, u32[]{:S(2)}, u32[]{:S(2)}) async-start(bf16[32,2,200]{2,1,0:T(2,128)(2,1)} %reshape.124), calls=%async_computation.2 | async-start | bytes 65536 | tf_op jit(solution)/shard_map/all_to_all | solution.py:46
  361.4 0.8 copy-start.1
  371.5 22.1 %all-to-all-start.1 = ((bf16[32,2,3328]{2,1,0:T(2,128)(2,1)}), bf16[32,2,3328]{2,1,0:T(2,128)(2,1)S(1)}, u32[]{:S(2)}, u32[]{:S(2)}) async-start(bf16[32,2,3328]{2,1,0:T(2,128)(2,1)} %reshape.122), calls=%async_computation.1 | async-start | bytes 851968 | tf_op jit(solution)/shard_map/all_to_all | solution.py:44
Sparse Core Ops, SparseCore 0:
  10.9 188.8 all-reduce.1
